TPU v7x, 256 devices: a whole 4x4x8 slice. The times are simulated.
256 devices in a mesh: dp: 16 (over y, x), expert: 16 (over z, core).
Axes of the slice: x: 4, y: 4, z: 8, core: 2. Of those that a mesh axis runs over, the one named last changes fastest.
Arguments:
- tokens: float32 [2048, 2048], P('expert'), may hold values from -6 to 6
- expert_ids: int32 [2048, 8], P('expert'), may hold values from 0 to 127, all different within a row; in each aligned block of 128 rows (0 to 127, 128 to 255, ...) at most 10 rows name the same one
- gate_values: float32 [2048, 8], P('expert'), may hold values from 0.05 to 1
- valid_mask: int32 [2048], P('expert'), may hold values from 0 to 1, as said below
- gate_weight: bfloat16 [128, 1536, 2048], P('expert', 'dp'), may hold values from -0.125 to 0.125
- up_weight: bfloat16 [128, 1536, 2048], P('expert', 'dp'), may hold values from -0.125 to 0.125
- down_weight: bfloat16 [128, 1536, 2048], P('expert', 'dp'), may hold values from -0.15625 to 0.15625
Outputs:
- blended: float32 [2048, 2048], P('expert')
- loss: float32 [], replicated
Inputs may be any that keep to these rules, and one draw needn't show every extreme that they name: `expert_ids`: each row names 8 different experts; in the 128 rows of one block no expert is named more than 10 times. `valid_mask`: each block of 128 tokens holds at least one valid token.
All inputs are finite; a program needn't handle non-finite values.
Results may differ from a plain program's by a relative error of at most 0.0058.
Values may be sent and summed in bfloat16 or wider, within the bound.
A program may use at most 128 MiB of HBM per device.

v0:
```python
import jax
import jax.numpy as jnp
from jax import lax
from jax.sharding import PartitionSpec as P

SLOTS = 16


def on_device(tokens, expert_ids, gate_values, valid_mask, gate_weight, up_weight, down_weight):
    tok_count, width = tokens.shape
    local_experts = gate_weight.shape[0]
    blocks = lax.axis_size("expert")
    parts = lax.axis_size("dp")
    piece = width // parts
    me = lax.axis_index("expert")
    part = lax.axis_index("dp")
    weights = valid_mask.astype(jnp.float32)
    mine = lax.dynamic_slice(tokens, (0, part * piece), (tok_count, piece)).astype(jnp.bfloat16)
    column = lax.all_gather(mine, "expert", axis=0, tiled=True)
    every = lax.all_gather(column, "dp", axis=1, tiled=True)
    ids = lax.all_gather(expert_ids, "expert", axis=0, tiled=True)
    gates = lax.all_gather(gate_values * weights[:, None], "expert", axis=0, tiled=True)
    local = me * local_experts + jnp.arange(local_experts, dtype=jnp.int32)
    match = ids[:, None, :] == local[None, :, None]
    named = jnp.any(match, axis=2)
    gate = jnp.sum(jnp.where(match, gates[:, None, :], 0.0), axis=2).reshape(
        blocks, tok_count, local_experts
    )
    taken = named.astype(jnp.int32).reshape(blocks, tok_count, local_experts)
    rank = jnp.cumsum(taken, axis=1) - taken
    pick = (
        rank.transpose(0, 2, 1)[:, :, None, :]
        == jnp.arange(SLOTS, dtype=jnp.int32)[None, None, :, None]
    ) & (taken.transpose(0, 2, 1)[:, :, None, :] > 0)
    slot_gate = jnp.sum(jnp.where(pick, gate.transpose(0, 2, 1)[:, :, None, :], 0.0), axis=3)
    pick = pick.astype(jnp.bfloat16)
    rows = jnp.einsum(
        "best,btf->ebsf",
        pick,
        every.reshape(blocks, tok_count, width),
        preferred_element_type=jnp.float32,
    ).astype(jnp.bfloat16)
    rows = rows.reshape(local_experts, blocks * SLOTS, width)
    gate_pre = jnp.einsum("erd,efd->erf", rows, gate_weight, preferred_element_type=jnp.float32)
    up_pre = jnp.einsum("erd,efd->erf", rows, up_weight, preferred_element_type=jnp.float32)
    hidden = (jax.nn.silu(gate_pre) * up_pre).astype(jnp.bfloat16)
    out = jnp.einsum("erf,efd->erd", hidden, down_weight, preferred_element_type=jnp.float32)
    out = (
        out.reshape(local_experts, blocks, SLOTS, width)
        * slot_gate.transpose(1, 0, 2)[:, :, :, None]
    )
    mixed = jnp.einsum(
        "best,ebsf->btf", pick, out.astype(jnp.bfloat16), preferred_element_type=jnp.float32
    ).reshape(blocks * tok_count, width)
    summed = lax.psum_scatter(mixed.astype(jnp.bfloat16), "dp", scatter_dimension=1, tiled=True)
    own = lax.psum_scatter(summed.astype(jnp.float32), "expert", scatter_dimension=0, tiled=True)
    blended = lax.all_gather(own, "dp", axis=1, tiled=True)
    per_token = jnp.mean(blended * blended, axis=1)
    local_loss = jnp.sum(per_token * weights)
    loss_sum, token_total = lax.psum((local_loss, jnp.sum(weights)), "expert")
    return (blended, loss_sum / token_total)


def solution(mesh):
    return jax.shard_map(
        on_device,
        mesh=mesh,
        in_specs=(
            P("expert", None),
            P("expert", None),
            P("expert", None),
            P("expert"),
            P("expert", "dp", None),
            P("expert", "dp", None),
            P("expert", "dp", None),
        ),
        out_specs=(P("expert", None), P()),
        check_vma=False,
    )
```

profile of v0, /device:TPU:1, one launch (start us, length us, event | category | flops | bytes accessed | tf_op | source)
XLA Modules:
  0.0 415.1 jit_solution(1104938401888615248)
XLA Ops:
  7.2 0.0 copy-start
  7.2 0.0 all-gather.3.cloned.1.call-start
  7.2 1.0 dynamic-slice_convert_fusion
  8.2 24.1 %all_gather.16 = bf16[2048,128]{1,0:T(8,128)(2,1)} all-gather(bf16[128,128]{1,0:T(8,128)(2,1)S(1)} %dynamic-slice_convert_fusion), channel_id=1, replica_groups=mesh['dp'=16,'expert'=16] {'expert'}, dimensions={0}, use_global_device_ids=true | all-gather | bytes 557056 | tf_op jit(solution)/shard_map/all_gather | solution.py:19
  32.3 0.0 all-gather.3.cloned.1.call-update
  32.4 0.0 reduce-scatter.7.cloned.1.call-start
  32.4 0.7 convert_element_type.41
  33.1 14.9 %all_gather.15 = s32[2048,8]{0,1:T(8,128)S(1)} all-gather(s32[128,8]{0,1:T(8,128)} %param.8), channel_id=1, replica_groups=mesh['dp'=16,'expert'=16] {'expert'}, dimensions={0}, use_global_device_ids=true | all-gather | bytes 69632 | tf_op jit(solution)/shard_map/all_gather | solution.py:21
  47.9 0.2 compare_reduce_fusion
  48.2 1.4 copy.28
  49.6 2.8 subtract_bitcast_fusion
  52.4 1.6 copy.30
  54.0 0.7 broadcast_multiply_fusion
  54.7 15.9 %all_gather.18 = f32[2048,8]{0,1:T(8,128)S(1)} all-gather(f32[128,8]{0,1:T(8,128)S(1)} %broadcast_multiply_fusion), channel_id=1, replica_groups=mesh['dp'=16,'expert'=16] {'expert'}, dimensions={0}, use_global_device_ids=true | all-gather | bytes 69632 | tf_op jit(solution)/shard_map/all_gather | solution.py:22
  70.6 0.2 fusion.16
  70.9 0.4 select_reduce_fusion
  71.3 39.7 %all-gather.3.cloned.1.call-done = bf16[2048,2048]{1,0:T(8,128)(2,1)} async-done(((bf16[2048,128]{1,0:T(8,128)(2,1)}), bf16[2048,2048]{1,0:T(8,128)(2,1)}) %all-gather.3.cloned.1.call-update) | async-done | bytes 8388624 | tf_op jit(solution)/shard_map/all_gather | solution.py:20
  111.0 8.9 %convert_bitcast_fusion = bf16[8,16,16,2048]{3,2,0,1:T(8,128)(2,1)} fusion(bf16[16,128,2048,1]{2,1,3,0:T(8,128)(2,1)} %bitcast.42, s32[16,8,128]{2,1,0:T(8,128)S(1)} %copy.30, pred[16,8,128]{2,1,0:T(8,128)(4,1)S(1)} %compare_bitcast_fusion), kind=kOutput, calls=%fused_computation.5 | convolution fusion | flops 1078460416 | bytes 16859136 | tf_op jit(solution)/shard_map/best,btf->ebsf/dot_general | solution.py:37
  119.9 0.0 copy-start.3
  119.9 8.4 %copy.31 = bf16[8,16,16,2048]{3,2,1,0:T(8,128)(2,1)} copy(bf16[8,16,16,2048]{3,2,0,1:T(8,128)(2,1)} %convert_bitcast_fusion) | data formatting | bytes 16777216 | tf_op jit(solution)/shard_map/convert_element_type | solution.py:42
  128.3 0.0 copy-done.3
  128.3 7.0 %fusion.23 = f32[8,256,96]{1,2,0:T(8,128)} fusion(bf16[8,256,2048]{2,1,0:T(8,128)(2,1)} %bitcast.37, bf16[8,96,2048]{2,1,0:T(8,128)(2,1)S(1)} %copy-done.3), kind=kOutput, calls=%fused_computation.35 | convolution fusion | flops 805306368 | bytes 12320768 | tf_op jit(solution)/shard_map/erd,efd->erf/dot_general | solution.py:44
  135.3 0.0 copy-done
  135.3 15.4 %fusion.7 = f32[8,256,2048]{2,1,0:T(8,128)} fusion(bf16[8,96,2048]{2,1,0:T(8,128)(2,1)S(1)} %copy-done, bf16[8,256,2048]{2,1,0:T(8,128)(2,1)} %bitcast.38, bf16[8,96,2048]{2,1,0:T(8,128)(2,1)} %param.12, f32[8,256,96]{1,2,0:T(8,128)} %fusion.23), kind=kOutput, calls=%fused_computation.8 | convolution fusion | flops 1611792384 | bytes 32243712 | tf_op jit(solution)/shard_map/erf,efd->erd/dot_general | solution.py:47
  150.7 11.4 %bitcast_convert_fusion = bf16[16,128,2048]{2,1,0:T(8,128)(2,1)} fusion(f32[8,16,16,2048]{3,2,1,0:T(8,128)} %bitcast.34, f32[8,16,16]{2,0,1:T(8,128)S(1)} %bitcast.40, s32[16,8,128]{2,1,0:T(8,128)S(1)} %copy.30, pred[16,8,128]{2,1,0:T(8,128)(4,1)S(1)} %compare_bitcast_fusion), kind=kOutput, calls=%fused_computation | convolution fusion | flops 1086849024 | bytes 25255936 | tf_op jit(solution)/shard_map/best,ebsf->btf/dot_general | solution.py:52
  162.1 0.0 copy-start.1
  162.1 12.5 %copy.35 = bf16[2048,2048]{0,1:T(8,128)(2,1)} copy(bf16[2048,2048]{1,0:T(8,128)(2,1)} %bitcast.36) | data formatting | bytes 16777216
  174.6 0.0 copy-start.2
  174.6 0.0 reduce-scatter.7.cloned.1.call-update
  174.6 0.0 reduce-scatter.5.cloned.1.call-start
  174.7 90.3 %reduce-scatter.7.cloned.1.call-done = bf16[128,2048]{1,0:T(8,128)(2,1)} async-done(((bf16[2048,2048]{1,0:T(8,128)(2,1)}), bf16[128,2048]{1,0:T(8,128)(2,1)}) %reduce-scatter.7.cloned.1.call-update) | async-done | bytes 524304
  265.0 2.0 copy.36
  267.0 2.1 convert_element_type.45
  269.1 0.0 reduce-scatter.5.cloned.1.call-update
  269.1 0.0 all-gather.5.cloned.1.call-start
  269.1 56.4 %reduce-scatter.5.cloned.1.call-done = f32[128,128]{1,0:T(8,128)} async-done(((f32[2048,128]{1,0:T(8,128)}), f32[128,128]{1,0:T(8,128)}) %reduce-scatter.5.cloned.1.call-update) | async-done | bytes 65552 | tf_op jit(solution)/shard_map/reduce_scatter | solution.py:56
  325.6 0.0 all-gather.5.cloned.1.call-update
  325.6 50.0 %all-gather.5.cloned.1.call-done = f32[128,2048]{1,0:T(8,128)} async-done(((f32[128,128]{1,0:T(8,128)}), f32[128,2048]{1,0:T(8,128)}) %all-gather.5.cloned.1.call-update) | async-done | bytes 1048592 | tf_op jit(solution)/shard_map/all_gather | solution.py:57
  375.5 1.4 multiply_reduce_fusion
  376.9 0.0 copy-done.2
  376.9 0.6 convert_reduce_fusion
  377.5 26.3 %all-reduce = (f32[]{:T(128)}, f32[]{:T(128)}) all-reduce(f32[]{:T(128)} %get-tuple-element.3, f32[]{:T(128)} %get-tuple-element.2), channel_id=1, replica_groups=mesh['dp'=16,'expert'=16] {'expert'}, use_global_device_ids=true, to_apply=%region_8.9 | all-reduce | flops 2 | bytes 16 | tf_op jit(solution)/shard_map/psum | solution.py:60
  405.1 2.3 copy.44
  407.4 0.0 copy-done.1
  (3 shorter events, 0.0 us)
Async XLA Ops:
  7.2 128.2 %copy-start = (bf16[8,96,2048]{2,1,0:T(8,128)(2,1)S(1)}, bf16[8,96,2048]{2,1,0:T(8,128)(2,1)}, u32[]{:S(2)}) copy-start(bf16[8,96,2048]{2,1,0:T(8,128)(2,1)} %param.13) | copy-start | bytes 9437188
  7.2 103.8 %all-gather.3.cloned.1.call-start = ((), (), s32[]{:S(2)}) async-start(), calls=%async_computation.2 | async-start | bytes 8912896 | tf_op jit(solution)/shard_map/all_gather | solution.py:20
  32.4 232.6 %reduce-scatter.7.cloned.1.call-start = ((), (), s32[]{:S(2)}) async-start(), calls=%async_computation.5 | async-start | bytes 8912896
  119.9 8.4 %copy-start.3 = (bf16[8,96,2048]{2,1,0:T(8,128)(2,1)S(1)}, bf16[8,96,2048]{2,1,0:T(8,128)(2,1)}, u32[]{:S(2)}) copy-start(bf16[8,96,2048]{2,1,0:T(8,128)(2,1)} %param.11) | copy-start | bytes 9437188
  162.1 245.3 %copy-start.1 = (bf16[8,96,2048]{2,1,0:T(8,128)(2,1)S(1)}, bf16[8,96,2048]{2,1,0:T(8,128)(2,1)}, u32[]{:S(2)}) copy-start(bf16[8,96,2048]{2,1,0:T(8,128)(2,1)} %param.13) | copy-start | bytes 9437188
  174.6 202.3 %copy-start.2 = (s32[128]{0:T(128)S(1)}, s32[128]{0:T(128)}, u32[]{:S(2)}) copy-start(s32[128]{0:T(128)} %param.10) | copy-start | bytes 1540
  174.6 150.9 %reduce-scatter.5.cloned.1.call-start = ((), (), s32[]{:S(2)}) async-start(), calls=%async_computation.3 | async-start | bytes 1114112 | tf_op jit(solution)/shard_map/reduce_scatter | solution.py:56
  269.1 106.5 %all-gather.5.cloned.1.call-start = ((), (), s32[]{:S(2)}) async-start(), calls=%async_computation.4 | async-start | bytes 1114112 | tf_op jit(solution)/shard_map/all_gather | solution.py:57
Sparse Core Ops, SparseCore 0:
  32.5 78.4 all-gather.2
  174.8 90.1 reduce-scatter.6
  269.2 56.2 reduce-scatter.4
  327.8 47.6 all-gather.4
where the time goes:
time: 416 us; the launch traced here: 415 us
  waiting for transfers between devices  236 us (57%)
  blocking collectives  81.2 us (20%)
  matrix products  42.7 us (10%)
  local copies, waits for them, and re-layouts  29.2 us (7%)
  between operations  16.3 us (4%)
  other arithmetic  9.13 us (2%)
    unnamed x5, waiting for transfers between devices  90.3 us
    reduce_scatter x1, waiting for transfers between devices, on_device(): lax.psum_scatter(summed.astype(jnp.float32), 'expert', scatter_dimension=...  56.4 us
    all_gather x1, waiting for transfers between devices, on_device(): blended = lax.all_gather(own, 'dp', axis=1, tiled=True)  50 us
    all_gather x1, waiting for transfers between devices, on_device(): every = lax.all_gather(column, 'dp', axis=1, tiled=True)  39.7 us
    psum x1, blocking collectives, on_device(): loss_sum, token_total = lax.psum((local_loss, jnp.sum(weights)), 'expert')  26.3 us
    all_gather x1, blocking collectives, on_device(): column = lax.all_gather(mine, 'expert', axis=0, tiled=True)  24.1 us
    unnamed x11, local copies, waits for them, and re-layouts  16.8 us
    all_gather x1, blocking collectives, on_device(): lax.all_gather(gate_values * weights[:, None], 'expert', axis=0, tiled=True)  15.9 us
  transfers between devices with their start and end apart: 4, of which 4 were waited for; matrix products, arithmetic and copies ran while one was open for 2% of the time, Pallas kernels for 0%

commit v1 on v0

--- a/solution.py
+++ b/solution.py
@@ -54,7 +54,9 @@
     ).reshape(blocks * tok_count, width)
     summed = lax.psum_scatter(mixed.astype(jnp.bfloat16), "dp", scatter_dimension=1, tiled=True)
     own = lax.psum_scatter(summed.astype(jnp.float32), "expert", scatter_dimension=0, tiled=True)
-    blended = lax.all_gather(own, "dp", axis=1, tiled=True)
+    blended = jnp.concatenate(
+        lax.all_to_all(jnp.stack([own] * lax.axis_size("dp")), "dp", 0, 0), axis=1
+    )
     per_token = jnp.mean(blended * blended, axis=1)
     local_loss = jnp.sum(per_token * weights)
     loss_sum, token_total = lax.psum((local_loss, jnp.sum(weights)), "expert")

time: 416 us -> 392 us (0.942)
  waiting for transfers between devices: 236 us -> 187 us
  blocking collectives: 81.2 us -> 104 us
    all_gather x1 -> x0, waiting for transfers between devices: 50 us -> none  [on_device(): blended = lax.all_gather(own, 'dp', axis=1, tiled=True)]
    all_to_all x0 -> x1, blocking collectives: none -> 19.7 us  [on_device(): lax.all_to_all(jnp.stack([own] * lax.axis_size('dp')), 'dp', 0, 0)]
    unnamed x5 -> x4, waiting for transfers between devices: 90.3 us -> 90.3 us
  transfers between devices with their start and end apart: 4 -> 3, of which waited for: 4 -> 3; matrix products, arithmetic and copies ran while one was open for 2% -> 2% of each run, Pallas kernels for 0% -> 0%
where the time goes in v1:
time: 392 us; the launch traced here: 391 us
  waiting for transfers between devices  187 us (48%)
  blocking collectives  104 us (27%)
  matrix products  42.7 us (11%)
  local copies, waits for them, and re-layouts  32.8 us (8%)
  between operations  16.3 us (4%)
  other arithmetic  9.34 us (2%)
    unnamed x4, waiting for transfers between devices  90.3 us
    reduce_scatter x1, waiting for transfers between devices, on_device(): lax.psum_scatter(summed.astype(jnp.float32), 'expert', scatter_dimension=...  56.5 us
    all_gather x1, waiting for transfers between devices, on_device(): every = lax.all_gather(column, 'dp', axis=1, tiled=True)  39.7 us
    psum x1, blocking collectives, on_device(): loss_sum, token_total = lax.psum((local_loss, jnp.sum(weights)), 'expert')  29 us
    all_gather x1, blocking collectives, on_device(): column = lax.all_gather(mine, 'expert', axis=0, tiled=True)  24.1 us
    all_to_all x1, blocking collectives, on_device(): lax.all_to_all(jnp.stack([own] * lax.axis_size('dp')), 'dp', 0, 0)  19.7 us
    unnamed x11, local copies, waits for them, and re-layouts  16.9 us
    all_gather x1, blocking collectives, on_device(): lax.all_gather(gate_values * weights[:, None], 'expert', axis=0, tiled=True)  15.9 us
  transfers between devices with their start and end apart: 3, of which 3 were waited for; matrix products, arithmetic and copies ran while one was open for 2% of the time, Pallas kernels for 0%

profile of v1, /device:TPU:1, one launch (start us, length us, event | category | flops | bytes accessed | tf_op | source)
XLA Modules:
  0.0 391.4 jit_solution(9866477094055461407)
XLA Ops:
  7.2 0.0 copy-start
  7.2 0.0 all-gather.2.cloned.1.call-start
  7.2 1.0 dynamic-slice_convert_fusion
  8.2 24.1 %all_gather.13 = bf16[2048,128]{1,0:T(8,128)(2,1)} all-gather(bf16[128,128]{1,0:T(8,128)(2,1)S(1)} %dynamic-slice_convert_fusion), channel_id=1, replica_groups=mesh['dp'=16,'expert'=16] {'expert'}, dimensions={0}, use_global_device_ids=true | all-gather | bytes 557056 | tf_op jit(solution)/shard_map/all_gather | solution.py:19
  32.3 0.0 all-gather.2.cloned.1.call-update
  32.4 0.0 reduce-scatter.7.cloned.1.call-start
  32.4 0.7 convert_element_type.41
  33.1 14.9 %all_gather.12 = s32[2048,8]{0,1:T(8,128)S(1)} all-gather(s32[128,8]{0,1:T(8,128)} %param.8), channel_id=1, replica_groups=mesh['dp'=16,'expert'=16] {'expert'}, dimensions={0}, use_global_device_ids=true | all-gather | bytes 69632 | tf_op jit(solution)/shard_map/all_gather | solution.py:21
  47.9 0.2 compare_reduce_fusion
  48.2 1.4 copy.37
  49.6 2.8 subtract_bitcast_fusion
  52.4 1.6 copy.39
  54.0 0.7 broadcast_multiply_fusion
  54.7 15.9 %all_gather.15 = f32[2048,8]{0,1:T(8,128)S(1)} all-gather(f32[128,8]{0,1:T(8,128)S(1)} %broadcast_multiply_fusion), channel_id=1, replica_groups=mesh['dp'=16,'expert'=16] {'expert'}, dimensions={0}, use_global_device_ids=true | all-gather | bytes 69632 | tf_op jit(solution)/shard_map/all_gather | solution.py:22
  70.6 0.2 fusion.17
  70.9 0.4 select_reduce_fusion
  71.3 39.7 %all-gather.2.cloned.1.call-done = bf16[2048,2048]{1,0:T(8,128)(2,1)} async-done(((bf16[2048,128]{1,0:T(8,128)(2,1)}), bf16[2048,2048]{1,0:T(8,128)(2,1)}) %all-gather.2.cloned.1.call-update) | async-done | bytes 8388624 | tf_op jit(solution)/shard_map/all_gather | solution.py:20
  111.0 8.9 %convert_bitcast_fusion = bf16[8,16,16,2048]{3,2,0,1:T(8,128)(2,1)} fusion(bf16[16,128,2048,1]{2,1,3,0:T(8,128)(2,1)} %bitcast.49, s32[16,8,128]{2,1,0:T(8,128)S(1)} %copy.39, pred[16,8,128]{2,1,0:T(8,128)(4,1)S(1)} %compare_bitcast_fusion), kind=kOutput, calls=%fused_computation.5 | convolution fusion | flops 1078460416 | bytes 16859136 | tf_op jit(solution)/shard_map/best,btf->ebsf/dot_general | solution.py:37
  119.9 0.0 copy-start.3
  119.9 8.4 %copy.40 = bf16[8,16,16,2048]{3,2,1,0:T(8,128)(2,1)} copy(bf16[8,16,16,2048]{3,2,0,1:T(8,128)(2,1)} %convert_bitcast_fusion) | data formatting | bytes 16777216 | tf_op jit(solution)/shard_map/convert_element_type | solution.py:42
  128.3 0.0 copy-done.3
  128.3 7.0 %fusion.24 = f32[8,256,96]{1,2,0:T(8,128)} fusion(bf16[8,256,2048]{2,1,0:T(8,128)(2,1)} %bitcast.43, bf16[8,96,2048]{2,1,0:T(8,128)(2,1)S(1)} %copy-done.3), kind=kOutput, calls=%fused_computation.36 | convolution fusion | flops 805306368 | bytes 12320768 | tf_op jit(solution)/shard_map/erd,efd->erf/dot_general | solution.py:44
  135.3 0.0 copy-done
  135.3 15.4 %fusion.7 = f32[8,256,2048]{2,1,0:T(8,128)} fusion(bf16[8,96,2048]{2,1,0:T(8,128)(2,1)S(1)} %copy-done, bf16[8,256,2048]{2,1,0:T(8,128)(2,1)} %bitcast.44, bf16[8,96,2048]{2,1,0:T(8,128)(2,1)} %param.12, f32[8,256,96]{1,2,0:T(8,128)} %fusion.24), kind=kOutput, calls=%fused_computation.8 | convolution fusion | flops 1611792384 | bytes 32243712 | tf_op jit(solution)/shard_map/erf,efd->erd/dot_general | solution.py:47
  150.7 11.4 %bitcast_convert_fusion = bf16[16,128,2048]{2,1,0:T(8,128)(2,1)} fusion(f32[8,16,16,2048]{3,2,1,0:T(8,128)} %bitcast.40, f32[8,16,16]{2,0,1:T(8,128)S(1)} %bitcast.47, s32[16,8,128]{2,1,0:T(8,128)S(1)} %copy.39, pred[16,8,128]{2,1,0:T(8,128)(4,1)S(1)} %compare_bitcast_fusion), kind=kOutput, calls=%fused_computation | convolution fusion | flops 1086849024 | bytes 25255936 | tf_op jit(solution)/shard_map/best,ebsf->btf/dot_general | solution.py:52
  162.1 12.3 %copy.46 = bf16[2048,2048]{0,1:T(8,128)(2,1)} copy(bf16[2048,2048]{1,0:T(8,128)(2,1)} %bitcast.42) | data formatting | bytes 16777216
  174.5 0.0 copy-start.1
  174.5 0.0 copy-start.2
  174.5 0.0 reduce-scatter.7.cloned.1.call-update
  174.5 0.0 reduce-scatter.5.cloned.1.call-start
  174.5 90.3 %reduce-scatter.7.cloned.1.call-done = bf16[128,2048]{1,0:T(8,128)(2,1)} async-done(((bf16[2048,2048]{1,0:T(8,128)(2,1)}), bf16[128,2048]{1,0:T(8,128)(2,1)}) %reduce-scatter.7.cloned.1.call-update) | async-done | bytes 524304
  264.8 2.0 copy.47
  266.8 2.1 convert_element_type.45
  268.9 0.0 reduce-scatter.5.cloned.1.call-update
  268.9 56.5 %reduce-scatter.5.cloned.1.call-done = f32[128,128]{1,0:T(8,128)} async-done(((f32[2048,128]{1,0:T(8,128)}), f32[128,128]{1,0:T(8,128)}) %reduce-scatter.5.cloned.1.call-update) | async-done | bytes 65552 | tf_op jit(solution)/shard_map/reduce_scatter | solution.py:56
  325.4 0.9 stack.2
  326.4 19.7 %all_to_all.5 = f32[16,128,128]{2,1,0:T(8,128)} all-to-all(f32[16,128,128]{2,1,0:T(8,128)S(1)} %stack.2), channel_id=1, replica_groups=mesh['dp'=16,'expert'=16] {'dp'}, dimensions={0} | all-to-all | bytes 2097152 | tf_op jit(solution)/shard_map/all_to_all | solution.py:58
  346.1 2.6 copy.42
  348.6 1.5 fusion.8
  350.2 0.0 copy-done.2
  350.2 0.7 convert_reduce_fusion
  350.8 2.5 copy.43
  353.4 29.0 %all-reduce = (f32[]{:T(128)}, f32[]{:T(128)}) all-reduce(f32[]{:T(128)} %get-tuple-element.7, f32[]{:T(128)} %get-tuple-element.6), channel_id=1, replica_groups=mesh['dp'=16,'expert'=16] {'expert'}, use_global_device_ids=true, to_apply=%region_8.9 | all-reduce | flops 2 | bytes 16 | tf_op jit(solution)/shard_map/psum | solution.py:62
  383.8 0.0 copy-done.1
  (3 shorter events, 0.0 us)
Async XLA Ops:
  7.2 128.2 %copy-start = (bf16[8,96,2048]{2,1,0:T(8,128)(2,1)S(1)}, bf16[8,96,2048]{2,1,0:T(8,128)(2,1)}, u32[]{:S(2)}) copy-start(bf16[8,96,2048]{2,1,0:T(8,128)(2,1)} %param.13) | copy-start | bytes 9437188
  7.2 103.8 %all-gather.2.cloned.1.call-start = ((), (), s32[]{:S(2)}) async-start(), calls=%async_computation.3 | async-start | bytes 8912896 | tf_op jit(solution)/shard_map/all_gather | solution.py:20
  32.4 232.4 %reduce-scatter.7.cloned.1.call-start = ((), (), s32[]{:S(2)}) async-start(), calls=%async_computation.5 | async-start | bytes 8912896
  119.9 8.4 %copy-start.3 = (bf16[8,96,2048]{2,1,0:T(8,128)(2,1)S(1)}, bf16[8,96,2048]{2,1,0:T(8,128)(2,1)}, u32[]{:S(2)}) copy-start(bf16[8,96,2048]{2,1,0:T(8,128)(2,1)} %param.11) | copy-start | bytes 9437188
  174.5 209.3 %copy-start.1 = (bf16[8,96,2048]{2,1,0:T(8,128)(2,1)S(1)}, bf16[8,96,2048]{2,1,0:T(8,128)(2,1)}, u32[]{:S(2)}) copy-start(bf16[8,96,2048]{2,1,0:T(8,128)(2,1)} %param.13) | copy-start | bytes 9437188
  174.5 175.7 %copy-start.2 = (s32[128]{0:T(128)S(1)}, s32[128]{0:T(128)}, u32[]{:S(2)}) copy-start(s32[128]{0:T(128)} %param.10) | copy-start | bytes 1540
  174.5 150.9 %reduce-scatter.5.cloned.1.call-start = ((), (), s32[]{:S(2)}) async-start(), calls=%async_computation.4 | async-start | bytes 1114112 | tf_op jit(solution)/shard_map/reduce_scatter | solution.py:56
Sparse Core Ops, SparseCore 0:
  32.5 78.4 all-gather.1
  174.6 90.1 reduce-scatter.6
  269.1 56.2 reduce-scatter.4
